TPU v7x, 512 devices: a whole 4x4x16 slice. The times are simulated.
512 devices in a mesh: seq: 32 (over z, core), head: 16 (over x, y).
Axes of the slice: x: 4, y: 4, z: 16, core: 2. Of those that a mesh axis runs over, the one named last changes fastest.
Arguments:
- tokens: bfloat16 [8192, 4096], P('seq', 'head'), may hold values from -40 to 40
- norm_gain: float32 [4096], replicated, may hold values from 1.5 to 8
- w_qkv: bfloat16 [4096, 3, 2048], P(None, None, 'head'), may hold values from -0.09375 to 0.09375
- w_out: bfloat16 [2048, 4096], P('head'), may hold values from -0.75 to 0.75
- span_order: int32 [64], replicated, may hold values from 0 to 63, each once
- frame_id: int32 [8192], replicated, may hold values from 0 to 63, never falling along the last dimension, each value on 1 to 256 neighbouring positions
- camera_id: int32 [8192], replicated, may hold values from 0 to 5
Outputs:
- mixed: bfloat16 [8192, 4096], P('seq', 'head')
Inputs may be any that keep to these rules, and one draw needn't show every extreme that they name: `span_order`: each of the 64 spans appears once. `frame_id`: never falls along the sequence; every frame has 1 to 256 positions and one has exactly 256.
All inputs are finite; a program needn't handle non-finite values.
Results may differ from a plain program's by a relative error of at most 0.015.
The roundings to bfloat16 on the way count: a program that leaves them out, or rounds other values in their place, can miss the bound.
Values may be sent and summed in bfloat16 or wider, within the bound.
No kernel may reach another device: no remote copies, remote signals or barrier semaphores. Data moves between devices by JAX's collectives and lax.ppermute only.
A program may use at most 64 MiB of HBM per device.

v0:
```python
import jax
import jax.numpy as jnp
from jax import lax
from jax.sharding import PartitionSpec as P

D = 4096
HD = 128
epsilon = 1e-06
key_block = 1024


def stored_order(id_table, span_order):
    span_count = span_order.shape[0]
    return id_table.reshape(span_count, -1)[span_order].reshape(-1)


def visible_pairs(query_frames, query_cameras, key_frames, key_cameras):
    earlier = key_frames[None, :] < query_frames[:, None]
    same_view = (key_frames[None, :] == query_frames[:, None]) & (
        key_cameras[None, :] == query_cameras[:, None]
    )
    return earlier | same_view


def on_device(tokens, norm_gain, w_qkv, w_out, span_order, frame_id, camera_id):
    gathered = lax.all_gather(tokens, "head", axis=1, tiled=True)
    widened = gathered.astype(jnp.float32)
    inverse = lax.rsqrt(jnp.mean(widened * widened, axis=1, keepdims=True) + epsilon)
    normed = (widened * inverse * norm_gain).astype(jnp.bfloat16)
    row_count = tokens.shape[0]
    local_heads = w_out.shape[0] // HD
    projected = jnp.dot(
        normed, w_qkv.reshape(D, 3 * local_heads * HD), preferred_element_type=jnp.float32
    )
    projected = projected.astype(jnp.bfloat16).reshape(row_count, 3, local_heads, HD)
    queries = projected[:, 0]
    key_rows = projected[:, 1].reshape(row_count, local_heads * HD)
    value_rows = projected[:, 2].reshape(row_count, local_heads * HD)
    frames = stored_order(frame_id, span_order)
    cameras = stored_order(camera_id, span_order)
    first_row = lax.axis_index("seq") * row_count
    query_frames = lax.dynamic_slice_in_dim(frames, first_row, row_count, 0)
    query_cameras = lax.dynamic_slice_in_dim(cameras, first_row, row_count, 0)
    score_scale = HD ** (-0.5)

    def absorb(running, block_keys, block_values, key_start, frame_table, camera_table):
        key_count = block_keys.shape[0]
        key_frames = lax.dynamic_slice_in_dim(frame_table, key_start, key_count, 0)
        key_cameras = lax.dynamic_slice_in_dim(camera_table, key_start, key_count, 0)
        old_best, running_total, weighted = running
        scores = (
            jnp.einsum(
                "qhd,khd->hqk",
                queries,
                block_keys.reshape(key_count, local_heads, HD),
                preferred_element_type=jnp.float32,
            )
            * score_scale
        )
        allowed = visible_pairs(query_frames, query_cameras, key_frames, key_cameras)[None]
        block_best = jnp.max(jnp.where(allowed, scores, -jnp.inf), axis=2)
        new_best = jnp.maximum(old_best, block_best)
        weights = jnp.exp(jnp.where(allowed, scores - new_best[:, :, None], -jnp.inf))
        factor = jnp.exp(old_best - new_best)
        running_total = running_total * factor + jnp.sum(weights, axis=2)
        added = jnp.einsum(
            "hqk,khd->hqd",
            weights.astype(jnp.bfloat16),
            block_values.reshape(key_count, local_heads, HD),
            preferred_element_type=jnp.float32,
        )
        weighted = weighted * factor[:, :, None] + added
        return (new_best, running_total, weighted)

    initial = (
        jnp.full((local_heads, row_count), -1e30, jnp.float32),
        jnp.zeros((local_heads, row_count), jnp.float32),
        jnp.zeros((local_heads, row_count, HD), jnp.float32),
    )
    all_keys, all_values = (
        lax.all_gather(key_rows, "seq", axis=0, tiled=True),
        lax.all_gather(value_rows, "seq", axis=0, tiled=True),
    )
    running = initial
    length = all_keys.shape[0]
    block_rows = min(key_block, length)
    full_blocks = length // block_rows

    def advance(block_index, current):
        offset = block_index * block_rows
        block_keys = lax.dynamic_slice_in_dim(all_keys, offset, block_rows, 0)
        block_values = lax.dynamic_slice_in_dim(all_values, offset, block_rows, 0)
        return absorb(current, block_keys, block_values, 0 + offset, frames, cameras)

    running = lax.fori_loop(0, full_blocks, advance, running)
    attended = (running[2] / running[1][:, :, None]).astype(jnp.bfloat16)
    partial_value = jnp.einsum(
        "hqd,hde->qe",
        attended,
        w_out.reshape(local_heads, HD, D),
        preferred_element_type=jnp.float32,
    )
    mixed_rows = lax.psum_scatter(
        partial_value.astype(jnp.bfloat16), "head", scatter_dimension=1, tiled=True
    )
    return mixed_rows


def solution(mesh):
    placed = (P("seq", "head"), P(), P(None, None, "head"), P("head", None), P(), P(), P())
    return jax.shard_map(
        on_device, mesh=mesh, in_specs=placed, out_specs=P("seq", "head"), check_vma=False
    )
```

profile of v0, /device:TPU:2, one launch (start us, length us, event | category | flops | bytes accessed | tf_op | source)
XLA Modules:
  0.0 355.3 jit_solution(11500444099656653798)
XLA Ops:
  6.5 0.0 copy-start
  6.5 0.0 all-gather.6.cloned.1.call-start
  6.5 0.7 all-gather.6.cloned.1.call-update
  7.3 0.0 all-gather.10.cloned.1.call-start
  7.3 0.0 copy-start.4
  7.3 4.7 %copy.11 = bf16[4096,3,128]{0,2,1:T(8,128)(2,1)} copy(bf16[4096,3,128]{2,0,1:T(8,128)(2,1)} %param.11) | data formatting | bytes 6291456 | tf_op args[2]
  12.0 64.8 %all-gather.6.cloned.1.call-done = bf16[256,4096]{1,0:T(8,128)(2,1)} async-done(((bf16[256,256]{1,0:T(8,128)(2,1)}), bf16[256,4096]{1,0:T(8,128)(2,1)}) %all-gather.6.cloned.1.call-update) | async-done | bytes 2097168 | tf_op jit(solution)/shard_map/all_gather | solution.py:26
  76.8 0.0 copy-start.3
  76.8 2.2 fusion.16
  79.1 0.0 copy-done.4
  79.1 0.0 copy-done.3
  79.1 0.0 copy-start.5
  79.1 0.0 copy-start.1
  79.1 0.0 copy-start.2
  79.1 3.3 fusion.23
  82.4 0.1 copy.12
  82.6 0.7 fusion.27
  83.2 0.0 all-gather.10.cloned.1.call-update
  83.3 0.0 all-gather.8.cloned.1.call-start
  83.3 0.7 all-gather.8.cloned.1.call-update
  84.0 0.0 reduce-scatter.2.cloned.1.call-start
  84.1 0.0 copy-done.5
  84.1 0.0 copy-done.1
  84.1 0.6 gather_fusion.1
  84.7 0.0 copy-done.2
  84.7 0.6 gather_fusion
  85.3 0.1 dynamic_slice.35
  85.4 0.1 dynamic_slice.34
  85.5 0.1 copy.13
  85.6 70.4 %all-gather.10.cloned.1.call-done = bf16[8192,1,1,128]{0,3,1,2:T(8,128)(2,1)} async-done(((bf16[256,1,1,128]{0,3,1,2:T(8,128)(2,1)}), bf16[8192,1,1,128]{0,3,1,2:T(8,128)(2,1)}) %all-gather.10.cloned.1.call-update) | async-done | bytes 2097168 | tf_op jit(solution)/shard_map/all_gather | solution.py:82
  156.0 70.8 %all-gather.8.cloned.1.call-done = bf16[8192,1,1,128]{0,3,1,2:T(8,128)(2,1)} async-done(((bf16[256,1,1,128]{0,3,1,2:T(8,128)(2,1)}), bf16[8192,1,1,128]{0,3,1,2:T(8,128)(2,1)}) %all-gather.8.cloned.1.call-update) | async-done | bytes 2097168 | tf_op jit(solution)/shard_map/all_gather | solution.py:81
  226.8 33.6 %while.18 = (s32[]{:T(128)}, f32[1,256]{1,0:T(1,128)S(1)}, f32[1,256]{1,0:T(1,128)S(1)}, f32[1,256,128]{2,1,0:T(8,128)S(1)}, s32[8192]{0:T(1024)S(1)}, /*index=5...) while((s32[]{:T(128)}, f32[1,256]{1,0:T(1,128)S(1)}, ...), condition=%wide.region_4.5_spmd.clone, body=%wide.region_1.4_spmd.clone.sunk | while | flops 140608768 | bytes 4061407 | solution.py:95
  226.8 1.7 select_reduce_fusion.2
  228.6 0.7 fusion.39
  229.3 1.7 fusion.41
  231.0 1.8 select_reduce_fusion.2
  232.8 0.7 fusion.39
  233.5 1.7 fusion.41
  235.3 1.8 select_reduce_fusion.2
  237.0 0.7 fusion.39
  237.7 1.7 fusion.41
  239.5 1.8 select_reduce_fusion.2
  241.3 0.7 fusion.39
  242.0 1.7 fusion.41
  243.7 1.8 select_reduce_fusion.2
  245.5 0.7 fusion.39
  246.2 1.7 fusion.41
  247.9 1.8 select_reduce_fusion.2
  249.7 0.7 fusion.39
  250.4 1.7 fusion.41
  252.1 1.8 select_reduce_fusion.2
  253.9 0.7 fusion.39
  254.6 1.7 fusion.41
  256.3 1.8 select_reduce_fusion.2
  258.1 0.7 fusion.39
  258.8 1.7 fusion.41
  260.5 0.0 copy-done
  260.5 2.1 convolution_convert_fusion
  262.6 0.0 reduce-scatter.2.cloned.1.call-update
  262.6 86.2 %reduce-scatter.2.cloned.1.call-done = bf16[256,256]{1,0:T(8,128)(2,1)} async-done(((bf16[256,4096]{1,0:T(8,128)(2,1)}), bf16[256,256]{1,0:T(8,128)(2,1)}) %reduce-scatter.2.cloned.1.call-update) | async-done | bytes 131088 | tf_op jit(solution)/shard_map/reduce_scatter | solution.py:103
  (46 shorter events, 0.4 us)
Async XLA Ops:
  6.5 254.0 %copy-start = (bf16[128,4096]{1,0:T(8,128)(2,1)S(1)}, bf16[128,4096]{1,0:T(8,128)(2,1)}, u32[]{:S(2)}) copy-start(bf16[128,4096]{1,0:T(8,128)(2,1)} %param.12) | copy-start | bytes 3145732
  6.5 70.3 %all-gather.6.cloned.1.call-start = ((), (), s32[]{:S(2)}) async-start(), calls=%async_computation.1 | async-start | bytes 2228224 | tf_op jit(solution)/shard_map/all_gather | solution.py:26
  7.3 148.8 %all-gather.10.cloned.1.call-start = ((), (), s32[]{:S(2)}) async-start(), calls=%async_computation.4 | async-start | bytes 2162688 | tf_op jit(solution)/shard_map/all_gather | solution.py:82
  7.3 71.7 %copy-start.4 = (f32[4096]{0:T(1024)S(1)}, f32[4096]{0:T(1024)}, u32[]{:S(2)}) copy-start(f32[4096]{0:T(1024)} %param.10) | copy-start | bytes 49156
  76.8 2.3 copy-start.3
  79.1 5.0 %copy-start.5 = (s32[64]{0:T(128)S(1)}, s32[64]{0:T(128)}, u32[]{:S(2)}) copy-start(s32[64]{0:T(128)} %param.13) | copy-start | bytes 772
  79.1 5.0 %copy-start.1 = (s32[8192]{0:T(1024)S(1)}, s32[8192]{0:T(1024)}, u32[]{:S(2)}) copy-start(s32[8192]{0:T(1024)} %param.15) | copy-start | bytes 98308
  79.1 5.6 %copy-start.2 = (s32[8192]{0:T(1024)S(1)}, s32[8192]{0:T(1024)}, u32[]{:S(2)}) copy-start(s32[8192]{0:T(1024)} %param.14) | copy-start | bytes 98308
  83.3 143.6 %all-gather.8.cloned.1.call-start = ((), (), s32[]{:S(2)}) async-start(), calls=%async_computation.3 | async-start | bytes 2162688 | tf_op jit(solution)/shard_map/all_gather | solution.py:81
  84.0 264.8 %reduce-scatter.2.cloned.1.call-start = ((), (), s32[]{:S(2)}) async-start(), calls=%async_computation.2 | async-start | bytes 2228224 | tf_op jit(solution)/shard_map/reduce_scatter | solution.py:103
Sparse Core Ops, SparseCore 0:
  10.3 66.4 all-gather.5
  83.4 72.6 all-gather.9
  158.1 68.7 all-gather.7
  262.7 86.0 reduce-scatter.1
where the time goes:
time: 356 us; the launch traced here: 355 us
  waiting for transfers between devices  294 us (83%)
  matrix products  32.7 us (9%)
  between operations  13.3 us (4%)
  other arithmetic  7.89 us (2%)
  local copies, waits for them, and re-layouts  7.13 us (2%)
    reduce_scatter x1, waiting for transfers between devices, on_device(): lax.psum_scatter(partial_value.astype(jnp.bfloat16), 'head', scatter_dime...  86.2 us
    all_gather x1, waiting for transfers between devices, on_device(): lax.all_gather(key_rows, 'seq', axis=0, tiled=True)  70.8 us
    all_gather x1, waiting for transfers between devices, on_device(): lax.all_gather(value_rows, 'seq', axis=0, tiled=True)  70.4 us
    all_gather x1, waiting for transfers between devices, on_device(): gathered = lax.all_gather(tokens, 'head', axis=1, tiled=True)  64.8 us
    dot_general x8, matrix products, absorb(): jnp.einsum('qhd,khd->hqk', queries, block_keys.reshape(key_count, local_h...  14.1 us
    dot_general x8, matrix products, absorb(): jnp.einsum('hqk,khd->hqd', weights.astype(jnp.bfloat16), block_values.res...  13.2 us
  transfers between devices with their start and end apart: 4, of which 4 were waited for; matrix products, arithmetic and copies ran while one was open for 2% of the time, Pallas kernels for 0%

commit v1 on v0

--- a/solution.py
+++ b/solution.py
@@ -23,7 +23,9 @@
 
 
 def on_device(tokens, norm_gain, w_qkv, w_out, span_order, frame_id, camera_id):
-    gathered = lax.all_gather(tokens, "head", axis=1, tiled=True)
+    gathered = jnp.concatenate(
+        lax.all_to_all(jnp.stack([tokens] * lax.axis_size("head")), "head", 0, 0), axis=1
+    )
     widened = gathered.astype(jnp.float32)
     inverse = lax.rsqrt(jnp.mean(widened * widened, axis=1, keepdims=True) + epsilon)
     normed = (widened * inverse * norm_gain).astype(jnp.bfloat16)

time: 356 us -> 325 us (0.913)
  waiting for transfers between devices: 294 us -> 253 us
  starting transfers between devices: 0.12 us -> 9.65 us
  local copies, waits for them, and re-layouts: 7.13 us -> 10.9 us
    all_gather x1 -> x0, waiting for transfers between devices: 64.8 us -> none  [on_device(): gathered = lax.all_gather(tokens, 'head', axis=1, tiled=True)]
    all_to_all x0 -> x1, waiting for transfers between devices: none -> 20.6 us  [on_device(): lax.all_to_all(jnp.stack([tokens] * lax.axis_size('head')), 'head', 0, 0)]
    all_to_all x0 -> x1, starting transfers between devices: none -> 9.54 us  [on_device(): lax.all_to_all(jnp.stack([tokens] * lax.axis_size('head')), 'head', 0, 0)]
    all_gather x1, waiting for transfers between devices: 70.4 us -> 74.3 us  [on_device(): lax.all_gather(value_rows, 'seq', axis=0, tiled=True)]
where the time goes in v1:
time: 325 us
  waiting for transfers between devices  253 us (78%)
  matrix products  30.7 us (9%)
  between operations  13.3 us (4%)
  local copies, waits for them, and re-layouts  10.9 us (3%)
  starting transfers between devices  9.65 us (3%)
  other arithmetic  6.95 us (2%)
    reduce_scatter x1, waiting for transfers between devices, on_device(): lax.psum_scatter(partial_value.astype(jnp.bfloat16), 'head', scatter_dime...  86.3 us
    all_gather x1, waiting for transfers between devices, on_device(): lax.all_gather(value_rows, 'seq', axis=0, tiled=True)  74.3 us
    all_gather x1, waiting for transfers between devices, on_device(): lax.all_gather(key_rows, 'seq', axis=0, tiled=True)  70.8 us
    all_to_all x1, waiting for transfers between devices, on_device(): lax.all_to_all(jnp.stack([tokens] * lax.axis_size('head')), 'head', 0, 0)  20.6 us
    dot_general x8, matrix products, absorb(): jnp.einsum('qhd,khd->hqk', queries, block_keys.reshape(key_count, local_h...  14.1 us
    dot_general x8, matrix products, absorb(): jnp.einsum('hqk,khd->hqd', weights.astype(jnp.bfloat16), block_values.res...  13.2 us
    all_to_all x1, starting transfers between devices, on_device(): lax.all_to_all(jnp.stack([tokens] * lax.axis_size('head')), 'head', 0, 0)  9.54 us
    unnamed x14, local copies, waits for them, and re-layouts  6.99 us
  transfers between devices with their start and end apart: 4, of which 4 were waited for; matrix products, arithmetic and copies ran while one was open for 2% of the time, Pallas kernels for 0%

profile of v1, /device:TPU:2, one launch (start us, length us, event | category | flops | bytes accessed | tf_op | source)
XLA Modules:
  0.0 324.7 jit_solution(229078291699532727)
XLA Ops:
  6.5 0.0 copy-start
  6.5 1.1 copy.11
  7.6 1.5 stack.2
  9.2 0.0 copy-start.4
  9.2 9.5 %all-to-all-start = ((bf16[16,256,256]{1,2,0:T(8,128)(2,1)}), bf16[16,256,256]{1,2,0:T(8,128)(2,1)S(1)}, u32[]{:S(2)}, u32[]{:S(2)}) async-start(bf16[16,256,256]{1,2,0:T(8,128)(2,1)} %stack.2), calls=%async_computation | async-start | bytes 4194304 | tf_op jit(solution)/shard_map/all_to_all | solution.py:27
  18.7 0.0 all-gather.7.cloned.1.call-start
  18.8 0.0 copy-done.4
  18.8 4.7 %copy.12 = bf16[4096,3,128]{0,2,1:T(8,128)(2,1)} copy(bf16[4096,3,128]{2,0,1:T(8,128)(2,1)} %param.11) | data formatting | bytes 6291456 | tf_op args[2]
  23.5 20.6 %all-to-all-done = bf16[16,256,256]{1,2,0:T(8,128)(2,1)S(1)} async-done(((bf16[16,256,256]{1,2,0:T(8,128)(2,1)}), bf16[16,256,256]{1,2,0:T(8,128)(2,1)S(1)}, u32[]{:S(2)}, u32[]{:S(2)}) %all-to-all-start) | async-done | bytes 2097184 | tf_op jit(solution)/shard_map/all_to_all | solution.py:27
  44.1 0.6 fusion.16
  44.7 0.0 copy-start.1
  44.7 0.7 fusion.18
  45.4 1.2 copy-done.1
  46.6 0.0 copy-start.5
  46.6 0.0 copy-start.2
  46.6 0.0 copy-start.3
  46.6 1.3 convolution_convert_fusion.1
  47.9 0.1 copy.13
  48.0 0.7 fusion.20
  48.7 0.0 all-gather.7.cloned.1.call-update
  48.7 0.0 all-gather.5.cloned.1.call-start
  48.7 0.7 all-gather.5.cloned.1.call-update
  49.4 0.0 reduce-scatter.2.cloned.1.call-start
  49.5 0.0 copy-done.5
  49.6 0.0 copy-done.2
  49.6 0.6 gather_fusion.1
  50.2 0.0 copy-done.3
  50.2 0.6 gather_fusion
  50.8 0.1 dynamic_slice.35
  50.8 0.1 dynamic_slice.34
  50.9 0.1 copy.14
  51.0 74.3 %all-gather.7.cloned.1.call-done = bf16[8192,1,1,128]{0,3,1,2:T(8,128)(2,1)} async-done(((bf16[256,1,1,128]{0,3,1,2:T(8,128)(2,1)}), bf16[8192,1,1,128]{0,3,1,2:T(8,128)(2,1)}) %all-gather.7.cloned.1.call-update) | async-done | bytes 2097168 | tf_op jit(solution)/shard_map/all_gather | solution.py:84
  125.4 70.8 %all-gather.5.cloned.1.call-done = bf16[8192,1,1,128]{0,3,1,2:T(8,128)(2,1)} async-done(((bf16[256,1,1,128]{0,3,1,2:T(8,128)(2,1)}), bf16[8192,1,1,128]{0,3,1,2:T(8,128)(2,1)}) %all-gather.5.cloned.1.call-update) | async-done | bytes 2097168 | tf_op jit(solution)/shard_map/all_gather | solution.py:83
  196.2 33.6 %while.18 = (s32[]{:T(128)}, f32[1,256]{1,0:T(1,128)S(1)}, f32[1,256]{1,0:T(1,128)S(1)}, f32[1,256,128]{2,1,0:T(8,128)S(1)}, s32[8192]{0:T(1024)S(1)}, /*index=5...) while((s32[]{:T(128)}, f32[1,256]{1,0:T(1,128)S(1)}, ...), condition=%wide.region_4.5_spmd.clone, body=%wide.region_1.4_spmd.clone.sunk | while | flops 140608768 | bytes 4061407 | solution.py:97
  196.2 1.7 select_reduce_fusion.2
  197.9 0.7 fusion.33
  198.6 1.7 fusion.35
  200.4 1.8 select_reduce_fusion.2
  202.2 0.7 fusion.33
  202.9 1.7 fusion.35
  204.6 1.8 select_reduce_fusion.2
  206.4 0.7 fusion.33
  207.1 1.7 fusion.35
  208.8 1.8 select_reduce_fusion.2
  210.6 0.7 fusion.33
  211.3 1.7 fusion.35
  213.0 1.8 select_reduce_fusion.2
  214.8 0.7 fusion.33
  215.5 1.7 fusion.35
  217.2 1.8 select_reduce_fusion.2
  219.0 0.7 fusion.33
  219.7 1.7 fusion.35
  221.4 1.8 select_reduce_fusion.2
  223.2 0.7 fusion.33
  223.9 1.7 fusion.35
  225.6 1.8 select_reduce_fusion.2
  227.4 0.7 fusion.33
  228.1 1.7 fusion.35
  229.8 0.0 copy-done
  229.8 2.1 convolution_convert_fusion
  231.9 0.0 reduce-scatter.2.cloned.1.call-update
  231.9 86.3 %reduce-scatter.2.cloned.1.call-done = bf16[256,256]{1,0:T(8,128)(2,1)} async-done(((bf16[256,4096]{1,0:T(8,128)(2,1)}), bf16[256,256]{1,0:T(8,128)(2,1)}) %reduce-scatter.2.cloned.1.call-update) | async-done | bytes 131088 | tf_op jit(solution)/shard_map/reduce_scatter | solution.py:105
  (47 shorter events, 0.4 us)
Async XLA Ops:
  6.5 223.3 %copy-start = (bf16[128,4096]{1,0:T(8,128)(2,1)S(1)}, bf16[128,4096]{1,0:T(8,128)(2,1)}, u32[]{:S(2)}) copy-start(bf16[128,4096]{1,0:T(8,128)(2,1)} %param.12) | copy-start | bytes 3145732
  9.2 9.6 %copy-start.4 = (f32[4096]{0:T(1024)S(1)}, f32[4096]{0:T(1024)}, u32[]{:S(2)}) copy-start(f32[4096]{0:T(1024)} %param.10) | copy-start | bytes 49156
  9.2 34.9 %all-to-all-start = ((bf16[16,256,256]{1,2,0:T(8,128)(2,1)}), bf16[16,256,256]{1,2,0:T(8,128)(2,1)S(1)}, u32[]{:S(2)}, u32[]{:S(2)}) async-start(bf16[16,256,256]{1,2,0:T(8,128)(2,1)} %stack.2), calls=%async_computation | async-start | bytes 4194304 | tf_op jit(solution)/shard_map/all_to_all | solution.py:27
  18.7 106.7 %all-gather.7.cloned.1.call-start = ((), (), s32[]{:S(2)}) async-start(), calls=%async_computation.4 | async-start | bytes 2162688 | tf_op jit(solution)/shard_map/all_gather | solution.py:84
  44.7 1.9 copy-start.1
  46.6 3.0 copy-start.5
  46.6 3.0 copy-start.2
  46.6 3.6 %copy-start.3 = (s32[8192]{0:T(1024)S(1)}, s32[8192]{0:T(1024)}, u32[]{:S(2)}) copy-start(s32[8192]{0:T(1024)} %param.14) | copy-start | bytes 98308
  48.7 147.5 %all-gather.5.cloned.1.call-start = ((), (), s32[]{:S(2)}) async-start(), calls=%async_computation.3 | async-start | bytes 2162688 | tf_op jit(solution)/shard_map/all_gather | solution.py:83
  49.4 268.8 %reduce-scatter.2.cloned.1.call-start = ((), (), s32[]{:S(2)}) async-start(), calls=%async_computation.2 | async-start | bytes 2228224 | tf_op jit(solution)/shard_map/reduce_scatter | solution.py:105
Sparse Core Ops, SparseCore 0:
  48.8 76.5 all-gather.6
  127.4 68.7 all-gather.4
  232.1 86.0 reduce-scatter.1
